TPU v7x, 32 devices: a whole 2x2x4 slice. The times are simulated.
32 devices in a mesh: dp: 16 (over z, x, core), mp: 2 (over y).
Axes of the slice: x: 2, y: 2, z: 4, core: 2. Of those that a mesh axis runs over, the one named last changes fastest.
Arguments:
- frames_in: float32 [12288, 768], P(('dp', 'mp')), may hold values from -6 to 6
- frames_cot: float32 [12288, 768], P(('dp', 'mp')), may hold values from -6 to 6
- clip_ids: int32 [12288], replicated, may hold values from 0 to 16, never falling along the last dimension, each value on 1 to 768 neighbouring positions
- frame_mask: int32 [12288], replicated, may hold values 0 or 1
- norm_gain: float32 [2, 2, 768], replicated, may hold values from 0.25 to 1.75
- norm_bias: float32 [2, 2, 768], replicated, may hold values from -2 to 2
- qkv_weight: bfloat16 [2, 768, 3, 768], P(None, 'dp', None, 'mp'), as said below
- qv_bias: float32 [2, 2, 768], P(None, None, 'mp'), may hold values from -0.4 to 0.4
- proj_weight: bfloat16 [2, 768, 768], P(None, ('mp', 'dp')), may hold values from -4 to 4
- up_weight: bfloat16 [2, 768, 3072], P(None, 'dp', 'mp'), may hold values from -0.21875 to 0.21875
- up_bias: float32 [2, 3072], P(None, 'mp'), may hold values from -3 to 3
- down_weight: bfloat16 [2, 3072, 768], P(None, ('mp', 'dp')), may hold values from -0.109375 to 0.109375
- out_biases: float32 [2, 2, 768], replicated, may hold values from -2 to 2
Outputs:
- frames_out: float32 [12288, 768], P(('dp', 'mp'))
- frames_grad: float32 [12288, 768], P(('dp', 'mp'))
- grad_qkv: float32 [2, 768, 3, 768], P(None, 'dp', None, 'mp')
- grad_qv_bias: float32 [2, 2, 768], P(None, None, 'mp')
- grad_proj: float32 [2, 768, 768], P(None, ('mp', 'dp'))
- grad_up: float32 [2, 768, 3072], P(None, 'dp', 'mp')
- grad_up_bias: float32 [2, 3072], P(None, 'mp')
- grad_down: float32 [2, 3072, 768], P(None, ('mp', 'dp'))
- grad_gain: float32 [2, 2, 768], replicated
- grad_norm_bias: float32 [2, 2, 768], replicated
- grad_out_biases: float32 [2, 2, 768], replicated
Inputs may be any that keep to these rules, and one draw needn't show every extreme that they name: `clip_ids`: clip numbers never fall from one frame to the next; each clip holds 1 to 768 frames and one holds exactly 768. `qkv_weight`: projection weights for queries, keys and values.
All inputs are finite; a program needn't handle non-finite values.
Results may differ from a plain program's by a relative error of at most 0.013.
Values may be sent and summed in bfloat16 or wider, within the bound.
A program may use at most 320 MiB of HBM per device.

v0:
```python
import jax
import jax.numpy as jnp
from jax import lax
from jax.sharding import PartitionSpec as P

HD = 64
epsilon = 1e-05


def padded_2(block, sides, width):
    for axis, dim in sides:
        count = lax.axis_size(axis)
        forward = [(i, i + 1) for i in range(count - 1)]
        backward = [(target, source) for source, target in forward]
        low = lax.ppermute(
            lax.slice_in_dim(block, block.shape[dim] - width, None, axis=dim), axis, forward
        )
        high = lax.ppermute(lax.slice_in_dim(block, 0, width, axis=dim), axis, backward)
        block = jnp.concatenate([low, block, high], axis=dim)
    return block


def shifted(x, axis, by):
    size = lax.axis_size(axis)
    pairs = [(i, i + by) for i in range(size) if 0 <= i + by < size]
    return lax.ppermute(x, axis, pairs)


def norm_forward(values, gain_vec, bias_vec):
    row_mean = jnp.mean(values, axis=-1, keepdims=True)
    centred = values - row_mean
    inverse = lax.rsqrt(jnp.mean(centred * centred, axis=-1, keepdims=True) + epsilon)
    normed = centred * inverse
    return ((normed * gain_vec + bias_vec).astype(jnp.bfloat16), normed, inverse)


def norm_backward(grad_out, normed, inverse, gain_vec):
    scaled = grad_out * gain_vec
    projected = (
        scaled
        - jnp.mean(scaled, axis=-1, keepdims=True)
        - normed * jnp.mean(scaled * normed, axis=-1, keepdims=True)
    )
    return (inverse * projected, jnp.sum(grad_out * normed, axis=0), jnp.sum(grad_out, axis=0))


def gelu_value(preact):
    return 0.5 * preact * (1.0 + jax.scipy.special.erf(preact * 0.7071067811865476))


def gelu_slope(preact):
    return (
        0.5 * (1.0 + jax.scipy.special.erf(preact * 0.7071067811865476))
        + preact * jnp.exp(-0.5 * preact * preact) * 0.3989422804014327
    )


def padded(values, tok_span, fill):
    border = jnp.full((tok_span,) + values.shape[1:], fill, values.dtype)
    return jnp.concatenate([border, values, border], axis=0)


def block_mask(query_ids, block_start, key_ids, key_valid, tok_span):
    query_pos = block_start + jnp.arange(query_ids.shape[0], dtype=jnp.int32)
    key_pos = jnp.arange(key_ids.shape[0], dtype=jnp.int32)
    same_clip = query_ids[:, None] == key_ids[None, :]
    visible = (key_valid[None, :] == 1) | (key_pos[None, :] == query_pos[:, None] + tok_span)
    return same_clip & visible


def window_ids(clip_ids, frame_mask, tok_span):
    offset = lax.axis_index("dp") * tok_span
    ids_pad = padded(clip_ids, tok_span, -1)
    valid_pad = padded(frame_mask, tok_span, 0)
    return (
        lax.dynamic_slice_in_dim(ids_pad, offset + tok_span, tok_span, 0),
        lax.dynamic_slice_in_dim(ids_pad, offset, 3 * tok_span, 0),
        lax.dynamic_slice_in_dim(valid_pad, offset, 3 * tok_span, 0),
    )


def fetch_weights(qkv_weight, proj_weight, up_weight, down_weight, depth):
    return (
        lax.all_gather(qkv_weight[depth], "dp", axis=0, tiled=True),
        lax.all_gather(proj_weight[depth], "dp", axis=0, tiled=True),
        lax.all_gather(up_weight[depth], "dp", axis=0, tiled=True),
        lax.all_gather(down_weight[depth], "dp", axis=0, tiled=True),
    )


def gather_rows(values):
    return lax.all_gather(values, "mp", axis=0, tiled=True)


def sum_rows(left, right):
    return lax.psum_scatter(
        jnp.dot(left, right, preferred_element_type=jnp.float32),
        "mp",
        scatter_dimension=0,
        tiled=True,
    )


def block_scores(query, keys, query_ids, key_ids, key_valid, offset):
    tok_span = query.shape[0]
    allowed = block_mask(query_ids, offset, key_ids, key_valid, tok_span)
    scores = jnp.einsum("qhd,khd->hqk", query, keys, preferred_element_type=jnp.float32) * HD ** (
        -0.5
    )
    return (query, jnp.where(allowed[None], scores, -1e30))


def attend(query, key_vals, query_ids, key_ids, key_valid):
    tok_span = query.shape[0]
    n_blocks = (tok_span + 1023) // 1024
    block_rows = tok_span // n_blocks
    keys = key_vals[:, 0]
    values = key_vals[:, 1]

    def one_block(block_id):
        offset = block_id * block_rows
        query_block, scores = block_scores(query, keys, query_ids, key_ids, key_valid, offset)
        row_max = jnp.max(scores, axis=-1, keepdims=True)
        log_total = row_max + jnp.log(jnp.sum(jnp.exp(scores - row_max), axis=-1, keepdims=True))
        prob_low = jnp.exp(scores - log_total).astype(jnp.bfloat16)
        attended = jnp.einsum(
            "hqk,khd->qhd", prob_low, values, preferred_element_type=jnp.float32
        ).astype(jnp.bfloat16)
        return (attended, log_total[..., 0])

    attended, log_totals = lax.map(one_block, jnp.arange(n_blocks, dtype=jnp.int32))
    return (attended.reshape(query.shape), log_totals)


def attend_back(query, key_vals, attended, grad_attn, log_totals, query_ids, key_ids, key_valid):
    tok_span = query.shape[0]
    n_blocks = (tok_span + 1023) // 1024
    block_rows = tok_span // n_blocks
    score_scale = HD ** (-0.5)
    keys = key_vals[:, 0]
    values = key_vals[:, 1]

    def one_block(key_grads, block_id):
        offset = block_id * block_rows
        query_block, scores = block_scores(query, keys, query_ids, key_ids, key_valid, offset)
        prob_full = jnp.exp(scores - log_totals[block_id][..., None])
        prob_low = prob_full.astype(jnp.bfloat16)
        grad_prob = jnp.einsum(
            "qhd,khd->hqk", grad_attn, values, preferred_element_type=jnp.float32
        )
        delta_row = jnp.sum(grad_attn.astype(jnp.float32) * attended.astype(jnp.float32), axis=-1).T
        score_low = (prob_full * (grad_prob - delta_row[..., None])).astype(jnp.bfloat16)
        grad_query = (
            jnp.einsum("hqk,khd->qhd", score_low, keys, preferred_element_type=jnp.float32)
            * score_scale
        )
        grad_key = (
            jnp.einsum("hqk,qhd->khd", score_low, query_block, preferred_element_type=jnp.float32)
            * score_scale
        )
        grad_value = jnp.einsum(
            "hqk,qhd->khd", prob_low, grad_attn, preferred_element_type=jnp.float32
        )
        return (key_grads + jnp.stack([grad_key, grad_value], axis=1), grad_query)

    start = jnp.zeros((3 * tok_span, 2) + query.shape[1:], jnp.float32)
    key_grads, grad_query = lax.scan(one_block, start, jnp.arange(n_blocks, dtype=jnp.int32))
    return (grad_query.reshape(query.shape), key_grads)


def widen(piece, full_width, mp_index):
    out_shape = piece.shape[:-1] + (full_width,)
    return lax.dynamic_update_slice_in_dim(
        jnp.zeros(out_shape, jnp.float32), piece, mp_index * piece.shape[-1], piece.ndim - 1
    )


def layer_forward(
    state, matrices, gain_pair, bias_pair, qv_pair, up_vec, out_pair, query_ids, key_ids, key_valid
):
    qkv_mat, proj_mat, up_mat, down_mat = matrices
    head_cols = qkv_mat.shape[-1]
    first_norm, hat_one, inv_one = norm_forward(state, gain_pair[0], bias_pair[0])
    first_full = gather_rows(first_norm)
    tok_span = first_full.shape[0]
    bias_three = jnp.stack([qv_pair[0], jnp.zeros_like(qv_pair[0]), qv_pair[1]])
    qkv_proj = jnp.dot(
        first_full,
        qkv_mat.reshape(qkv_mat.shape[0], 3 * head_cols),
        preferred_element_type=jnp.float32,
    )
    qkv_proj = (qkv_proj.reshape(tok_span, 3, head_cols) + bias_three).astype(jnp.bfloat16)
    query = qkv_proj[:, 0].reshape(tok_span, head_cols // HD, HD)
    key_vals = qkv_proj[:, 1:].reshape(tok_span, 2 * head_cols)
    key_vals = padded_2(key_vals, (("dp", 0),), tok_span)
    key_vals = key_vals.reshape(3 * tok_span, 2, head_cols // HD, HD)
    attended, log_totals = attend(query, key_vals, query_ids, key_ids, key_valid)
    attn_flat = attended.reshape(tok_span, head_cols)
    middle = state + sum_rows(attn_flat, proj_mat) + out_pair[0]
    second_norm, hat_two, inv_two = norm_forward(middle, gain_pair[1], bias_pair[1])
    second_full = gather_rows(second_norm)
    preact = jnp.dot(second_full, up_mat, preferred_element_type=jnp.float32) + up_vec
    hidden = gelu_value(preact).astype(jnp.bfloat16)
    result = middle + sum_rows(hidden, down_mat) + out_pair[1]
    stored = {
        "hat_one": hat_one,
        "inv_one": inv_one,
        "first_full": first_full,
        "query": query,
        "key_vals": key_vals,
        "attended": attended,
        "log_totals": log_totals,
        "hat_two": hat_two,
        "inv_two": inv_two,
        "second_full": second_full,
        "preact": preact,
        "hidden": hidden,
    }
    return (stored, result)


def layer_backward(gradient, stored, matrices, gain_pair, query_ids, key_ids, key_valid):
    qkv_mat, proj_mat, up_mat, down_mat = matrices
    head_cols = qkv_mat.shape[-1]
    grad_full = gather_rows(gradient.astype(jnp.bfloat16))
    grad_down = jnp.dot(stored["hidden"].T, grad_full, preferred_element_type=jnp.float32)
    grad_pre = jnp.dot(grad_full, down_mat.T, preferred_element_type=jnp.float32) * gelu_slope(
        stored["preact"]
    )
    grad_upb = jnp.sum(grad_pre, axis=0)
    pre_low = grad_pre.astype(jnp.bfloat16)
    grad_up = jnp.dot(stored["second_full"].T, pre_low, preferred_element_type=jnp.float32)
    grad_second = sum_rows(pre_low, up_mat.T)
    back_two, gain_two, shift_two = norm_backward(
        grad_second, stored["hat_two"], stored["inv_two"], gain_pair[1]
    )
    grad_middle = gradient + back_two
    middle_full = gather_rows(grad_middle.astype(jnp.bfloat16))
    attended = stored["attended"]
    tok_span = attended.shape[0]
    grad_proj = jnp.dot(
        attended.reshape(tok_span, head_cols).T, middle_full, preferred_element_type=jnp.float32
    )
    grad_attn = jnp.dot(middle_full, proj_mat.T, preferred_element_type=jnp.float32).astype(
        jnp.bfloat16
    )
    grad_attn = grad_attn.reshape(attended.shape)
    grad_query, key_grads = attend_back(
        stored["query"],
        stored["key_vals"],
        attended,
        grad_attn,
        stored["log_totals"],
        query_ids,
        key_ids,
        key_valid,
    )
    key_grads = key_grads.reshape(3 * tok_span, 2 * head_cols)
    own_grads = key_grads[tok_span : 2 * tok_span]
    for step_by, piece in ((1, key_grads[2 * tok_span :]), (-1, key_grads[:tok_span])):
        own_grads = own_grads + shifted(piece.astype(jnp.bfloat16), "dp", step_by).astype(
            piece.dtype
        )
    grad_query = grad_query.reshape(tok_span, head_cols)
    grad_key = own_grads[:, :head_cols]
    grad_value = own_grads[:, head_cols:]
    grad_qv = jnp.stack([jnp.sum(grad_query, axis=0), jnp.sum(grad_value, axis=0)])
    qkv_low = (
        jnp.stack([grad_query, grad_key, grad_value], axis=1)
        .astype(jnp.bfloat16)
        .reshape(tok_span, 3 * head_cols)
    )
    grad_qkv = jnp.dot(stored["first_full"].T, qkv_low, preferred_element_type=jnp.float32).reshape(
        -1, 3, head_cols
    )
    grad_first = sum_rows(qkv_low, qkv_mat.reshape(-1, 3 * head_cols).T)
    back_one, gain_one, shift_one = norm_backward(
        grad_first, stored["hat_one"], stored["inv_one"], gain_pair[0]
    )
    new_grad = grad_middle + back_one
    mp_index = lax.axis_index("mp")
    mp_count = lax.axis_size("mp")
    small = (
        jnp.stack([gain_one, gain_two]),
        jnp.stack([shift_one, shift_two]),
        jnp.stack([jnp.sum(grad_middle, axis=0), jnp.sum(gradient, axis=0)]),
        widen(grad_qv, head_cols * mp_count, mp_index),
        widen(grad_upb, grad_upb.shape[0] * mp_count, mp_index),
    )
    return (new_grad, (grad_qkv, grad_proj, grad_up, grad_down), small)


def body(
    frames_in,
    frames_cot,
    clip_ids,
    frame_mask,
    norm_gain,
    norm_bias,
    qkv_weight,
    qv_bias,
    proj_weight,
    up_weight,
    up_bias,
    down_weight,
    out_biases,
):
    layers = qkv_weight.shape[0]
    tok_span = frames_in.shape[0] * lax.axis_size("mp")
    query_ids, key_ids, key_valid = window_ids(clip_ids, frame_mask, tok_span)
    stored_all = []
    state = frames_in
    for depth in range(layers):
        matrices = fetch_weights(qkv_weight, proj_weight, up_weight, down_weight, depth)
        stored, state = layer_forward(
            state,
            matrices,
            norm_gain[depth],
            norm_bias[depth],
            qv_bias[depth],
            up_bias[depth],
            out_biases[depth],
            query_ids,
            key_ids,
            key_valid,
        )
        stored_all.append(stored)
    gradient = frames_cot
    weight_grads = []
    small_grads = []
    for depth in range(layers - 1, -1, -1):
        matrices = fetch_weights(qkv_weight, proj_weight, up_weight, down_weight, depth)
        gradient, mats_grad, small = layer_backward(
            gradient, stored_all[depth], matrices, norm_gain[depth], query_ids, key_ids, key_valid
        )
        mats_grad = (
            lax.psum_scatter(mats_grad[0], "dp", scatter_dimension=0, tiled=True),
            lax.psum_scatter(mats_grad[1], "dp", scatter_dimension=0, tiled=True),
            lax.psum_scatter(mats_grad[2], "dp", scatter_dimension=0, tiled=True),
            lax.psum_scatter(mats_grad[3], "dp", scatter_dimension=0, tiled=True),
        )
        small = lax.psum((small[0], small[1], small[2], small[3], small[4]), ("dp", "mp"))
        weight_grads.insert(0, mats_grad)
        small_grads.insert(0, small)
    stacked_w = tuple((jnp.stack([entry[slot] for entry in weight_grads]) for slot in range(4)))
    stacked_s = tuple((jnp.stack([entry[slot] for entry in small_grads]) for slot in range(5)))
    mp_index = lax.axis_index("mp")
    head_cols = qv_bias.shape[-1]
    up_cols = up_bias.shape[-1]
    grad_qv = lax.dynamic_slice_in_dim(stacked_s[3], mp_index * head_cols, head_cols, 2)
    grad_upb = lax.dynamic_slice_in_dim(stacked_s[4], mp_index * up_cols, up_cols, 1)
    return (
        state,
        gradient,
        stacked_w[0],
        grad_qv,
        stacked_w[1],
        stacked_w[2],
        grad_upb,
        stacked_w[3],
        stacked_s[0],
        stacked_s[1],
        stacked_s[2],
    )


def solution(mesh):
    placed = (
        P(("dp", "mp"), None),
        P(("dp", "mp"), None),
        P(),
        P(),
        P(),
        P(),
        P(None, "dp", None, "mp"),
        P(None, None, "mp"),
        P(None, ("mp", "dp"), None),
        P(None, "dp", "mp"),
        P(None, "mp"),
        P(None, ("mp", "dp"), None),
        P(),
    )
    return jax.shard_map(
        body,
        mesh=mesh,
        in_specs=placed,
        out_specs=(
            P(("dp", "mp"), None),
            P(("dp", "mp"), None),
            P(None, "dp", None, "mp"),
            P(None, None, "mp"),
            P(None, ("mp", "dp"), None),
            P(None, "dp", "mp"),
            P(None, "mp"),
            P(None, ("mp", "dp"), None),
            P(),
            P(),
            P(),
        ),
        check_vma=False,
    )
```

profile of v0, /device:TPU:0, one launch (start us, length us, event | category | flops | bytes accessed | tf_op | source)
XLA Modules:
  0.0 1947.3 jit_solution(16931985044161411071)
XLA Ops:
  14.8 39.2 %all-gather.39.cloned.1.call-done = bf16[1,768,3,384]{3,1,2,0:T(8,128)(2,1)} async-done(((bf16[1,48,3,384]{3,1,2,0:T(8,128)(2,1)}), bf16[1,768,3,384]{3,1,2,0:T(8,128)(2,1)}) %all-gather.39.cloned.1.call-update) | async-done | bytes 1769488 | tf_op jit(solution)/shard_map/all_gather | solution.py:84
  88.5 39.6 %all-gather.1 = bf16[1,384,768]{2,1,0:T(8,128)(2,1)} all-gather(bf16[1,24,768]{2,1,0:T(8,128)(2,1)S(1)} %get-tuple-element.207), channel_id=3, replica_groups=mesh['dp'=16,'mp'=2] {'dp'}, dimensions={1}, use_global_device_ids=true | all-gather | bytes 626688 | tf_op jit(solution)/shard_map/all_gather | solution.py:85
  198.3 32.1 %reduce-scatter.17.cloned.1.call-done = f32[384,768]{1,0:T(8,128)} async-done(((f32[768,768]{1,0:T(8,128)}), f32[384,768]{1,0:T(8,128)}) %reduce-scatter.17.cloned.1.call-update) | async-done | bytes 1179664 | tf_op jit(solution)/shard_map/reduce_scatter | solution.py:96
  235.6 39.8 %all-gather.41.cloned.1.call-done = bf16[1,768,1536]{2,1,0:T(8,128)(2,1)} async-done(((bf16[1,48,1536]{2,1,0:T(8,128)(2,1)}), bf16[1,768,1536]{2,1,0:T(8,128)(2,1)}) %all-gather.41.cloned.1.call-update) | async-done | bytes 2359312 | tf_op jit(solution)/shard_map/all_gather | solution.py:86
  275.4 23.5 %all-gather.25.cloned.1.call-done = bf16[768,768]{1,0:T(8,128)(2,1)} async-done(((bf16[384,768]{1,0:T(8,128)(2,1)}), bf16[768,768]{1,0:T(8,128)(2,1)}) %all-gather.25.cloned.1.call-update) | async-done | bytes 1179664 | tf_op jit(solution)/shard_map/all_gather | solution.py:92
  305.9 38.0 %all-gather.43.cloned.1.call-done = bf16[1,1536,768]{2,1,0:T(8,128)(2,1)} async-done(((bf16[1,96,768]{2,1,0:T(8,128)(2,1)}), bf16[1,1536,768]{2,1,0:T(8,128)(2,1)}) %all-gather.43.cloned.1.call-update) | async-done | bytes 2359312 | tf_op jit(solution)/shard_map/all_gather | solution.py:87
  350.5 32.9 %reduce-scatter.19.cloned.1.call-done = f32[384,768]{1,0:T(8,128)} async-done(((f32[768,768]{1,0:T(8,128)}), f32[384,768]{1,0:T(8,128)}) %reduce-scatter.19.cloned.1.call-update) | async-done | bytes 1179664 | tf_op jit(solution)/shard_map/reduce_scatter | solution.py:96
  387.1 39.1 %all-gather.45.cloned.1.call-done = bf16[1,768,3,384]{3,1,2,0:T(8,128)(2,1)} async-done(((bf16[1,48,3,384]{3,1,2,0:T(8,128)(2,1)}), bf16[1,768,3,384]{3,1,2,0:T(8,128)(2,1)}) %all-gather.45.cloned.1.call-update) | async-done | bytes 1769488 | tf_op jit(solution)/shard_map/all_gather | solution.py:84
  428.8 21.0 %all-gather.27.cloned.1.call-done = bf16[768,768]{1,0:T(8,128)(2,1)} async-done(((bf16[384,768]{1,0:T(8,128)(2,1)}), bf16[768,768]{1,0:T(8,128)(2,1)}) %all-gather.27.cloned.1.call-update) | async-done | bytes 1179664 | tf_op jit(solution)/shard_map/all_gather | solution.py:92
  457.2 39.2 %all-gather.5 = bf16[1,384,768]{2,1,0:T(8,128)(2,1)S(1)} all-gather(bf16[1,24,768]{2,1,0:T(8,128)(2,1)S(1)} %copy-done.50), channel_id=7, replica_groups=mesh['dp'=16,'mp'=2] {'dp'}, dimensions={1}, use_global_device_ids=true | all-gather | bytes 626688 | tf_op jit(solution)/shard_map/all_gather | solution.py:85
  557.9 33.6 %reduce-scatter.21.cloned.1.call-done = f32[384,768]{1,0:T(8,128)} async-done(((f32[768,768]{1,0:T(8,128)}), f32[384,768]{1,0:T(8,128)}) %reduce-scatter.21.cloned.1.call-update) | async-done | bytes 1179664 | tf_op jit(solution)/shard_map/reduce_scatter | solution.py:96
  599.2 37.5 %all-gather.47.cloned.1.call-done = bf16[1,768,1536]{2,1,0:T(8,128)(2,1)} async-done(((bf16[1,48,1536]{2,1,0:T(8,128)(2,1)}), bf16[1,768,1536]{2,1,0:T(8,128)(2,1)}) %all-gather.47.cloned.1.call-update) | async-done | bytes 2359312 | tf_op jit(solution)/shard_map/all_gather | solution.py:86
  636.7 23.5 %all-gather.29.cloned.1.call-done = bf16[768,768]{1,0:T(8,128)(2,1)} async-done(((bf16[384,768]{1,0:T(8,128)(2,1)}), bf16[768,768]{1,0:T(8,128)(2,1)}) %all-gather.29.cloned.1.call-update) | async-done | bytes 1179664 | tf_op jit(solution)/shard_map/all_gather | solution.py:92
  685.1 44.5 %all-gather.49.cloned.1.call-done = bf16[1,1536,768]{2,1,0:T(8,128)(2,1)} async-done(((bf16[1,96,768]{2,1,0:T(8,128)(2,1)}), bf16[1,1536,768]{2,1,0:T(8,128)(2,1)}) %all-gather.49.cloned.1.call-update) | async-done | bytes 2359312 | tf_op jit(solution)/shard_map/all_gather | solution.py:87
  746.7 27.8 %reduce-scatter.25.cloned.1.call-done = f32[384,768]{1,0:T(8,128)} async-done(((f32[768,768]{1,0:T(8,128)}), f32[384,768]{1,0:T(8,128)}) %reduce-scatter.25.cloned.1.call-update) | async-done | bytes 1179664 | tf_op jit(solution)/shard_map/reduce_scatter | solution.py:96
  777.9 33.6 %reduce-scatter.23.cloned.1.call-done = f32[384,768]{1,0:T(8,128)} async-done(((f32[768,768]{1,0:T(8,128)}), f32[384,768]{1,0:T(8,128)}) %reduce-scatter.23.cloned.1.call-update) | async-done | bytes 1179664 | tf_op jit(solution)/shard_map/reduce_scatter | solution.py:96
  818.3 22.4 %all-gather.33.cloned.1.call-done = bf16[768,768]{1,0:T(8,128)(2,1)} async-done(((bf16[384,768]{1,0:T(8,128)(2,1)}), bf16[768,768]{1,0:T(8,128)(2,1)}) %all-gather.33.cloned.1.call-update) | async-done | bytes 1179664 | tf_op jit(solution)/shard_map/all_gather | solution.py:92
  862.5 28.0 %multiply_convert_fusion.1 = bf16[6,768,2304]{2,1,0:T(8,128)(2,1)} fusion(f32[6,768,2304]{2,1,0:T(8,128)} %get-tuple-element.219, bf16[768,6,64]{0,2,1:T(8,128)(2,1)S(1)} %bitcast.283, f32[6,768]{1,0:T(8,128)S(1)} %bitcast.293, f32[6,768]{1,0:T(8,128)S(1)} %copy-done.74, pred[768,2304]{1,0:T(8,128)(4,1)S(1)} %fusion.7, ...), kind=kOutput, calls=%fused_computation.1 | convolution fusion | flops 1422655488 | bytes 67866624 | tf_op jit(solution)/shard_map/while/body/eval_jaxpr/qhd,khd->hqk/dot_general | solution.py:148
  941.3 41.2 %reduce-scatter.27.cloned.1.call-done = f32[384,768]{1,0:T(8,128)} async-done(((f32[768,768]{1,0:T(8,128)}), f32[384,768]{1,0:T(8,128)}) %reduce-scatter.27.cloned.1.call-update) | async-done | bytes 1179664 | tf_op jit(solution)/shard_map/reduce_scatter | solution.py:96
  988.1 22.9 %all-gather.35.cloned.1.call-done = bf16[768,768]{1,0:T(8,128)(2,1)} async-done(((bf16[384,768]{1,0:T(8,128)(2,1)}), bf16[768,768]{1,0:T(8,128)(2,1)}) %all-gather.35.cloned.1.call-update) | async-done | bytes 1179664 | tf_op jit(solution)/shard_map/all_gather | solution.py:92
  1022.2 34.9 %reduce-scatter.29.cloned.1.call-done = f32[384,768]{1,0:T(8,128)} async-done(((f32[768,768]{1,0:T(8,128)}), f32[384,768]{1,0:T(8,128)}) %reduce-scatter.29.cloned.1.call-update) | async-done | bytes 1179664 | tf_op jit(solution)/shard_map/reduce_scatter | solution.py:96
  1062.9 22.6 %all-gather.37.cloned.1.call-done = bf16[768,768]{1,0:T(8,128)(2,1)} async-done(((bf16[384,768]{1,0:T(8,128)(2,1)}), bf16[768,768]{1,0:T(8,128)(2,1)}) %all-gather.37.cloned.1.call-update) | async-done | bytes 1179664 | tf_op jit(solution)/shard_map/all_gather | solution.py:92
  1107.1 28.2 %multiply_convert_fusion = bf16[6,768,2304]{2,1,0:T(8,128)(2,1)} fusion(f32[6,768,2304]{2,1,0:T(8,128)} %get-tuple-element.215, bf16[768,6,64]{0,2,1:T(8,128)(2,1)S(1)} %bitcast.280, f32[6,768]{1,0:T(8,128)S(1)} %bitcast.292, f32[6,768]{1,0:T(8,128)S(1)} %copy-done.73, pred[768,2304]{1,0:T(8,128)(4,1)S(1)} %fusion.7, ...), kind=kOutput, calls=%fused_computation | convolution fusion | flops 1422655488 | bytes 67866624 | tf_op jit(solution)/shard_map/while/body/eval_jaxpr/qhd,khd->hqk/dot_general | solution.py:148
  1260.2 42.7 %reduce-scatter.47.cloned.1.call-done = f32[96,768]{1,0:T(8,128)} async-done(((f32[1536,768]{1,0:T(8,128)}), f32[96,768]{1,0:T(8,128)}) %reduce-scatter.47.cloned.1.call-update) | async-done | bytes 294928 | tf_op jit(solution)/shard_map/reduce_scatter | solution.py:340
  1302.9 78.5 %reduce-scatter.45.cloned.1.call-done = f32[96,768]{1,0:T(8,128)} async-done(((f32[1536,768]{1,0:T(8,128)}), f32[96,768]{1,0:T(8,128)}) %reduce-scatter.45.cloned.1.call-update) | async-done | bytes 294928 | tf_op jit(solution)/shard_map/reduce_scatter | solution.py:340
  1383.3 76.8 %reduce-scatter.43.cloned.1.call-done = f32[48,1536]{1,0:T(8,128)} async-done(((f32[768,1536]{1,0:T(8,128)}), f32[48,1536]{1,0:T(8,128)}) %reduce-scatter.43.cloned.1.call-update) | async-done | bytes 294928 | tf_op jit(solution)/shard_map/reduce_scatter | solution.py:339
  1460.1 78.5 %reduce-scatter.41.cloned.1.call-done = f32[48,1536]{1,0:T(8,128)} async-done(((f32[768,1536]{1,0:T(8,128)}), f32[48,1536]{1,0:T(8,128)}) %reduce-scatter.41.cloned.1.call-update) | async-done | bytes 294928 | tf_op jit(solution)/shard_map/reduce_scatter | solution.py:339
  1540.5 59.0 %reduce-scatter.39.cloned.1.call-done = f32[24,768]{1,0:T(8,128)} async-done(((f32[384,768]{1,0:T(8,128)}), f32[24,768]{1,0:T(8,128)}) %reduce-scatter.39.cloned.1.call-update) | async-done | bytes 73744 | tf_op jit(solution)/shard_map/reduce_scatter | solution.py:338
  1599.5 60.9 %reduce-scatter.37.cloned.1.call-done = f32[24,768]{1,0:T(8,128)} async-done(((f32[384,768]{1,0:T(8,128)}), f32[24,768]{1,0:T(8,128)}) %reduce-scatter.37.cloned.1.call-update) | async-done | bytes 73744 | tf_op jit(solution)/shard_map/reduce_scatter | solution.py:338
  1664.7 128.0 %all-reduce.3.cloned.1.call-done = (f32[1,2,768]{2,1,0:T(2,128)}, f32[1,2,768]{2,1,0:T(2,128)}, f32[1,3072]{1,0:T(1,128)}, f32[1,3072]{1,0:T(1,128)}, f32[1,2,76...) async-done(((f32[1,2,768]{2,1,0:T(2,128)}, f32[1,2,768]{2,1,0:T(2,128)}, ...) | async-done | bytes 73744 | tf_op jit(solution)/shard_map/psum | solution.py:342
  1799.2 68.4 %reduce-scatter.35.cloned.1.call-done = f32[48,3,384]{2,0,1:T(8,128)} async-done(((f32[768,3,384]{2,0,1:T(8,128)}), f32[48,3,384]{2,0,1:T(8,128)}) %reduce-scatter.35.cloned.1.call-update) | async-done | bytes 221200 | tf_op jit(solution)/shard_map/reduce_scatter | solution.py:337
  1867.6 70.9 %reduce-scatter.33.cloned.1.call-done = f32[48,3,384]{2,0,1:T(8,128)} async-done(((f32[768,3,384]{2,0,1:T(8,128)}), f32[48,3,384]{2,0,1:T(8,128)}) %reduce-scatter.33.cloned.1.call-update) | async-done | bytes 221200 | tf_op jit(solution)/shard_map/reduce_scatter | solution.py:337
  (444 shorter events, 523.2 us)
Async XLA Ops:
  9.0 68.7 %all-gather.23.cloned.1.call-start = ((), (), s32[]{:S(2)}) async-start(), calls=%async_computation.16 | async-start | bytes 1769472 | tf_op jit(solution)/shard_map/all_gather | solution.py:92
  13.4 217.0 %reduce-scatter.17.cloned.1.call-start = ((), (), s32[]{:S(2)}) async-start(), calls=%async_computation.17 | async-start | bytes 3538944 | tf_op jit(solution)/shard_map/reduce_scatter | solution.py:96
  82.9 49.3 %collective-permute-start.1 = (bf16[768,768]{0,1:T(8,128)(2,1)}, bf16[768,768]{0,1:T(8,128)(2,1)}, u32[]{:S(2)}, u32[]{:S(2)}) collective-permute-start(bf16[768,768]{0,1:T(8,128)(2,1)} %bitcast.6), channel_id=1, source_target_pairs={{2,0},{4,2},{6,4},{8,6},{10,8},{12,10},{14,12},{16,14},{18,16},{20... | collective-permute-start | bytes 3538952 | tf_op jit(solution)/shard_map/ppermute | solution.py:18
  84.2 48.0 %collective-permute-start = (bf16[768,768]{0,1:T(8,128)(2,1)}, bf16[768,768]{0,1:T(8,128)(2,1)}, u32[]{:S(2)}, u32[]{:S(2)}) collective-permute-start(bf16[768,768]{0,1:T(8,128)(2,1)} %bitcast.6), channel_id=1, source_target_pairs={{0,2},{2,4},{4,6},{6,8},{8,10},{10,12},{12,14},{14,16},{16,18},{18... | collective-permute-start | bytes 3538952 | tf_op jit(solution)/shard_map/ppermute | solution.py:15
  195.9 79.5 %all-gather.41.cloned.1.call-start = ((), (), s32[]{:S(2)}) async-start(), calls=%async_computation.41 | async-start | bytes 2506752 | tf_op jit(solution)/shard_map/all_gather | solution.py:86
  197.6 101.3 %all-gather.25.cloned.1.call-start = ((), (), s32[]{:S(2)}) async-start(), calls=%async_computation.18 | async-start | bytes 1769472 | tf_op jit(solution)/shard_map/all_gather | solution.py:92
  234.0 110.0 %all-gather.43.cloned.1.call-start = ((), (), s32[]{:S(2)}) async-start(), calls=%async_computation.42 | async-start | bytes 2506752 | tf_op jit(solution)/shard_map/all_gather | solution.py:87
  234.8 148.6 %reduce-scatter.19.cloned.1.call-start = ((), (), s32[]{:S(2)}) async-start(), calls=%async_computation.19 | async-start | bytes 3538944 | tf_op jit(solution)/shard_map/reduce_scatter | solution.py:96
  349.8 76.5 %all-gather.45.cloned.1.call-start = ((), (), s32[]{:S(2)}) async-start(), calls=%async_computation.43 | async-start | bytes 1880064 | tf_op jit(solution)/shard_map/all_gather | solution.py:84
  350.5 99.3 %all-gather.27.cloned.1.call-start = ((), (), s32[]{:S(2)}) async-start(), calls=%async_computation.20 | async-start | bytes 1769472 | tf_op jit(solution)/shard_map/all_gather | solution.py:92
  387.0 204.5 %reduce-scatter.21.cloned.1.call-start = ((), (), s32[]{:S(2)}) async-start(), calls=%async_computation.21 | async-start | bytes 3538944 | tf_op jit(solution)/shard_map/reduce_scatter | solution.py:96
  557.1 79.6 %all-gather.47.cloned.1.call-start = ((), (), s32[]{:S(2)}) async-start(), calls=%async_computation.44 | async-start | bytes 2506752 | tf_op jit(solution)/shard_map/all_gather | solution.py:86
  557.8 102.4 %all-gather.29.cloned.1.call-start = ((), (), s32[]{:S(2)}) async-start(), calls=%async_computation.22 | async-start | bytes 1769472 | tf_op jit(solution)/shard_map/all_gather | solution.py:92
  595.1 90.0 %all-gather.31.cloned.1.call-start = ((), (), s32[]{:S(2)}) async-start(), calls=%async_computation.24 | async-start | bytes 1769472 | tf_op jit(solution)/shard_map/all_gather | solution.py:92
  598.4 131.2 %all-gather.49.cloned.1.call-start = ((), (), s32[]{:S(2)}) async-start(), calls=%async_computation.45 | async-start | bytes 2506752 | tf_op jit(solution)/shard_map/all_gather | solution.py:87
  598.9 175.6 %reduce-scatter.25.cloned.1.call-start = ((), (), s32[]{:S(2)}) async-start(), calls=%async_computation.25 | async-start | bytes 3538944 | tf_op jit(solution)/shard_map/reduce_scatter | solution.py:96
  740.8 70.6 %reduce-scatter.23.cloned.1.call-start = ((), (), s32[]{:S(2)}) async-start(), calls=%async_computation.23 | async-start | bytes 3538944 | tf_op jit(solution)/shard_map/reduce_scatter | solution.py:96
  746.7 94.0 %all-gather.33.cloned.1.call-start = ((), (), s32[]{:S(2)}) async-start(), calls=%async_computation.26 | async-start | bytes 1769472 | tf_op jit(solution)/shard_map/all_gather | solution.py:92
  817.8 164.6 %reduce-scatter.27.cloned.1.call-start = ((), (), s32[]{:S(2)}) async-start(), calls=%async_computation.27 | async-start | bytes 3538944 | tf_op jit(solution)/shard_map/reduce_scatter | solution.py:96
  941.2 69.7 %all-gather.35.cloned.1.call-start = ((), (), s32[]{:S(2)}) async-start(), calls=%async_computation.28 | async-start | bytes 1769472 | tf_op jit(solution)/shard_map/all_gather | solution.py:92
  988.0 69.0 %reduce-scatter.29.cloned.1.call-start = ((), (), s32[]{:S(2)}) async-start(), calls=%async_computation.29 | async-start | bytes 3538944 | tf_op jit(solution)/shard_map/reduce_scatter | solution.py:96
  1022.2 63.4 %all-gather.37.cloned.1.call-start = ((), (), s32[]{:S(2)}) async-start(), calls=%async_computation.30 | async-start | bytes 1769472 | tf_op jit(solution)/shard_map/all_gather | solution.py:92
  1062.7 179.0 %reduce-scatter.31.cloned.1.call-start = ((), (), s32[]{:S(2)}) async-start(), calls=%async_computation.31 | async-start | bytes 3538944 | tf_op jit(solution)/shard_map/reduce_scatter | solution.py:96
  1182.4 120.5 %reduce-scatter.47.cloned.1.call-start = ((), (), s32[]{:S(2)}) async-start(), calls=%async_computation.39 | async-start | bytes 5013504 | tf_op jit(solution)/shard_map/reduce_scatter | solution.py:340
  1189.5 191.9 %reduce-scatter.45.cloned.1.call-start = ((), (), s32[]{:S(2)}) async-start(), calls=%async_computation.38 | async-start | bytes 5013504 | tf_op jit(solution)/shard_map/reduce_scatter | solution.py:340
  1196.7 263.4 %reduce-scatter.43.cloned.1.call-start = ((), (), s32[]{:S(2)}) async-start(), calls=%async_computation.37 | async-start | bytes 5013504 | tf_op jit(solution)/shard_map/reduce_scatter | solution.py:339
  1203.9 334.7 %reduce-scatter.41.cloned.1.call-start = ((), (), s32[]{:S(2)}) async-start(), calls=%async_computation.36 | async-start | bytes 5013504 | tf_op jit(solution)/shard_map/reduce_scatter | solution.py:339
  1211.0 388.5 %reduce-scatter.39.cloned.1.call-start = ((), (), s32[]{:S(2)}) async-start(), calls=%async_computation.35 | async-start | bytes 1253376 | tf_op jit(solution)/shard_map/reduce_scatter | solution.py:338
  1214.1 446.2 %reduce-scatter.37.cloned.1.call-start = ((), (), s32[]{:S(2)}) async-start(), calls=%async_computation.34 | async-start | bytes 1253376 | tf_op jit(solution)/shard_map/reduce_scatter | solution.py:338
  1217.8 574.8 %all-reduce.3.cloned.1.call-start = ((), (), s32[]{:S(2)}) async-start(), calls=%async_computation.46 | async-start | bytes 147456 | tf_op jit(solution)/shard_map/psum | solution.py:342
  1246.0 621.6 %reduce-scatter.35.cloned.1.call-start = ((), (), s32[]{:S(2)}) async-start(), calls=%async_computation.33 | async-start | bytes 3760128 | tf_op jit(solution)/shard_map/reduce_scatter | solution.py:337
  1251.0 687.5 %reduce-scatter.33.cloned.1.call-start = ((), (), s32[]{:S(2)}) async-start(), calls=%async_computation.32 | async-start | bytes 3760128 | tf_op jit(solution)/shard_map/reduce_scatter | solution.py:337
  (104 other events, 3123.2 us)
Sparse Core Ops, SparseCore 0:
  10.9 43.1 all-gather.38
  56.2 21.4 all-gather.22
  196.0 34.2 reduce-scatter.16
  233.1 42.2 all-gather.40
  277.4 21.4 all-gather.24
  301.6 42.2 all-gather.42
  349.9 33.5 reduce-scatter.18
  385.7 40.4 all-gather.44
  428.3 21.4 all-gather.26
  557.2 34.2 reduce-scatter.20
  594.4 42.2 all-gather.46
  638.7 21.4 all-gather.28
  662.3 22.7 all-gather.30
  687.2 42.2 all-gather.48
  741.0 33.5 reduce-scatter.24
  776.6 34.7 reduce-scatter.22
  817.9 22.7 all-gather.32
  941.4 41.0 reduce-scatter.26
  988.2 22.7 all-gather.34
  1022.3 34.7 reduce-scatter.28
  1062.8 22.7 all-gather.36
  1182.5 40.8 reduce-scatter.30
  1227.3 75.5 reduce-scatter.46
  1306.6 74.7 reduce-scatter.44
  1385.3 74.7 reduce-scatter.42
  1463.8 74.7 reduce-scatter.40
  1542.1 57.3 reduce-scatter.38
  1603.1 57.1 reduce-scatter.36
  1667.9 124.6 all-reduce.2
  1796.3 71.2 reduce-scatter.34
  1871.5 66.9 reduce-scatter.32
where the time goes:
time: 1950 us
  waiting for transfers between devices  1310 us (67%)
  matrix products  312 us (16%)
  other arithmetic  129 us (7%)
  blocking collectives  78.8 us (4%)
  local copies, waits for them, and re-layouts  73.5 us (4%)
  starting transfers between devices  23.5 us (1%)
    reduce_scatter x8, waiting for transfers between devices, sum_rows(): lax.psum_scatter(jnp.dot(left, right, preferred_element_type=jnp.float32)...  236 us
    all_gather x8, waiting for transfers between devices, gather_rows(): return lax.all_gather(values, 'mp', axis=0, tiled=True)  175 us
    reduce_scatter x2, waiting for transfers between devices, body(): lax.psum_scatter(mats_grad[2], 'dp', scatter_dimension=0, tiled=True)  155 us
    reduce_scatter x2, waiting for transfers between devices, body(): lax.psum_scatter(mats_grad[0], 'dp', scatter_dimension=0, tiled=True)  139 us
    psum x1, waiting for transfers between devices, body(): lax.psum((small[0], small[1], small[2], small[3], small[4]), ('dp', 'mp'))  128 us
    reduce_scatter x2, waiting for transfers between devices, body(): lax.psum_scatter(mats_grad[3], 'dp', scatter_dimension=0, tiled=True)  121 us
    reduce_scatter x2, waiting for transfers between devices, body(): lax.psum_scatter(mats_grad[1], 'dp', scatter_dimension=0, tiled=True)  120 us
    all_gather x2, waiting for transfers between devices, fetch_weights(): lax.all_gather(down_weight[depth], 'dp', axis=0, tiled=True)  82.5 us
  transfers between devices with their start and end apart: 39, of which 30 were waited for; matrix products, arithmetic and copies ran while one was open for 9% of the time, Pallas kernels for 0%

commit v1 on v0

--- a/solution.py
+++ b/solution.py
@@ -89,7 +89,29 @@
 
 
 def gather_rows(values):
-    return lax.all_gather(values, "mp", axis=0, tiled=True)
+
+    def words_put(x_in):
+        group_axis = "mp"
+        tall, local_now, e_next = (
+            lax.axis_size(group_axis),
+            lax.axis_index(group_axis),
+            x_in.shape[0],
+        )
+        reply, new = (x_in, 1)
+        while new < tall:
+            reply = jnp.concatenate(
+                [
+                    reply,
+                    lax.ppermute(
+                        reply, group_axis, perm=[(jj, (jj - new) % tall) for jj in range(tall)]
+                    ),
+                ],
+                axis=0,
+            )
+            new = 2 * new
+        return jnp.roll(reply, local_now * e_next, axis=0)
+
+    return words_put(values)
 
 
 def sum_rows(left, right):

time: 1950 us -> 1840 us (0.944)
  waiting for transfers between devices: 1310 us -> 1170 us
  other arithmetic: 129 us -> 149 us
    all_gather x8 -> x0, waiting for transfers between devices: 175 us -> none  [gather_rows(): return lax.all_gather(values, 'mp', axis=0, tiled=True)]
    ppermute x0 -> x8, waiting for transfers between devices: none -> 84.3 us  [words_put(): lax.ppermute(reply, group_axis, perm=[(jj, (jj - new) % tall) for jj in r...]
    reduce_scatter x2, waiting for transfers between devices: 121 us -> 155 us  [body(): lax.psum_scatter(mats_grad[3], 'dp', scatter_dimension=0, tiled=True)]
    reduce_scatter x2, waiting for transfers between devices: 120 us -> 85.7 us  [body(): lax.psum_scatter(mats_grad[1], 'dp', scatter_dimension=0, tiled=True)]
    all_gather x2, waiting for transfers between devices: 77.2 us -> 43.3 us  [fetch_weights(): lax.all_gather(up_weight[depth], 'dp', axis=0, tiled=True)]
    concatenate x0 -> x5, other arithmetic: none -> 20.5 us  [words_put(): return jnp.roll(reply, local_now * e_next, axis=0)]
  transfers between devices with their start and end apart: 39 -> 39, of which waited for: 30 -> 28; matrix products, arithmetic and copies ran while one was open for 9% -> 10% of each run, Pallas kernels for 0% -> 0%
where the time goes in v1:
time: 1840 us; the launch traced here: 1830 us
  waiting for transfers between devices  1170 us (64%)
  matrix products  303 us (16%)
  other arithmetic  149 us (8%)
  local copies, waits for them, and re-layouts  87.4 us (5%)
  blocking collectives  79.2 us (4%)
  starting transfers between devices  29.5 us (2%)
    reduce_scatter x8, waiting for transfers between devices, sum_rows(): lax.psum_scatter(jnp.dot(left, right, preferred_element_type=jnp.float32)...  239 us
    reduce_scatter x2, waiting for transfers between devices, body(): lax.psum_scatter(mats_grad[3], 'dp', scatter_dimension=0, tiled=True)  155 us
    reduce_scatter x2, waiting for transfers between devices, body(): lax.psum_scatter(mats_grad[2], 'dp', scatter_dimension=0, tiled=True)  155 us
    reduce_scatter x2, waiting for transfers between devices, body(): lax.psum_scatter(mats_grad[0], 'dp', scatter_dimension=0, tiled=True)  139 us
    psum x1, waiting for transfers between devices, body(): lax.psum((small[0], small[1], small[2], small[3], small[4]), ('dp', 'mp'))  129 us
    reduce_scatter x2, waiting for transfers between devices, body(): lax.psum_scatter(mats_grad[1], 'dp', scatter_dimension=0, tiled=True)  85.7 us
    ppermute x8, waiting for transfers between devices, words_put(): lax.ppermute(reply, group_axis, perm=[(jj, (jj - new) % tall) for jj in r...  84.3 us
    all_gather x2, blocking collectives, fetch_weights(): lax.all_gather(proj_weight[depth], 'dp', axis=0, tiled=True)  79.2 us
  transfers between devices with their start and end apart: 39, of which 28 were waited for; matrix products, arithmetic and copies ran while one was open for 10% of the time, Pallas kernels for 0%

profile of v1, /device:TPU:0, one launch (start us, length us, event | category | flops | bytes accessed | tf_op | source)
XLA Modules:
  0.0 1830.3 jit_solution(3002592605052659240)
XLA Ops:
  33.9 20.1 %all-gather.15.cloned.1.call-done = bf16[1,768,3,384]{3,1,2,0:T(8,128)(2,1)} async-done(((bf16[1,48,3,384]{3,1,2,0:T(8,128)(2,1)}), bf16[1,768,3,384]{3,1,2,0:T(8,128)(2,1)}) %all-gather.15.cloned.1.call-update) | async-done | bytes 1769488 | tf_op jit(solution)/shard_map/all_gather | solution.py:84
  67.4 39.1 %all-gather.1 = bf16[1,384,768]{2,1,0:T(8,128)(2,1)} all-gather(bf16[1,24,768]{2,1,0:T(8,128)(2,1)S(1)} %get-tuple-element.208), channel_id=3, replica_groups=mesh['dp'=16,'mp'=2] {'dp'}, dimensions={1}, use_global_device_ids=true | all-gather | bytes 626688 | tf_op jit(solution)/shard_map/all_gather | solution.py:85
  114.2 18.2 fusion.2
  132.4 20.6 %exponential_reduce_fusion.1 = f32[6,768]{1,0:T(8,128)S(1)} fusion(f32[6,768,2304]{2,1,0:T(8,128)} %get-tuple-element.216, f32[6,768]{1,0:T(8,128)} %get-tuple-element.215, pred[768,2304]{1,0:T(8,128)(4,1)S(1)} %fusion.7), kind=kLoop, calls=%fused_computation.6 | loop fusion | flops 42462720 | bytes 44273664 | tf_op jit(solution)/shard_map/while/body/eval_jaxpr/reduce_sum | solution.py:146
  179.6 29.7 %reduce-scatter.17.cloned.1.call-done = f32[384,768]{1,0:T(8,128)} async-done(((f32[768,768]{1,0:T(8,128)}), f32[384,768]{1,0:T(8,128)}) %reduce-scatter.17.cloned.1.call-update) | async-done | bytes 1179664 | tf_op jit(solution)/shard_map/reduce_scatter | solution.py:118
  230.3 23.9 %all-gather.17.cloned.1.call-done = bf16[1,768,1536]{2,1,0:T(8,128)(2,1)} async-done(((bf16[1,48,1536]{2,1,0:T(8,128)(2,1)}), bf16[1,768,1536]{2,1,0:T(8,128)(2,1)}) %all-gather.17.cloned.1.call-update) | async-done | bytes 2359312 | tf_op jit(solution)/shard_map/all_gather | solution.py:86
  260.0 38.0 %all-gather.19.cloned.1.call-done = bf16[1,1536,768]{2,1,0:T(8,128)(2,1)} async-done(((bf16[1,96,768]{2,1,0:T(8,128)(2,1)}), bf16[1,1536,768]{2,1,0:T(8,128)(2,1)}) %all-gather.19.cloned.1.call-update) | async-done | bytes 2359312 | tf_op jit(solution)/shard_map/all_gather | solution.py:87
  304.7 32.8 %reduce-scatter.19.cloned.1.call-done = f32[384,768]{1,0:T(8,128)} async-done(((f32[768,768]{1,0:T(8,128)}), f32[384,768]{1,0:T(8,128)}) %reduce-scatter.19.cloned.1.call-update) | async-done | bytes 1179664 | tf_op jit(solution)/shard_map/reduce_scatter | solution.py:118
  340.7 39.9 %all-gather.21.cloned.1.call-done = bf16[1,768,3,384]{3,1,2,0:T(8,128)(2,1)} async-done(((bf16[1,48,3,384]{3,1,2,0:T(8,128)(2,1)}), bf16[1,768,3,384]{3,1,2,0:T(8,128)(2,1)}) %all-gather.21.cloned.1.call-update) | async-done | bytes 1769488 | tf_op jit(solution)/shard_map/all_gather | solution.py:84
  393.9 40.1 %all-gather.5 = bf16[1,384,768]{2,1,0:T(8,128)(2,1)} all-gather(bf16[1,24,768]{2,1,0:T(8,128)(2,1)S(1)} %copy-done.65), channel_id=7, replica_groups=mesh['dp'=16,'mp'=2] {'dp'}, dimensions={1}, use_global_device_ids=true | all-gather | bytes 626688 | tf_op jit(solution)/shard_map/all_gather | solution.py:85
  436.0 17.7 fusion.3
  453.7 19.9 %exponential_reduce_fusion = f32[6,768]{1,0:T(8,128)S(1)} fusion(f32[6,768,2304]{2,1,0:T(8,128)} %get-tuple-element.220, f32[6,768]{1,0:T(8,128)S(1)} %get-tuple-element.219, pred[768,2304]{1,0:T(8,128)(4,1)S(1)} %fusion.7), kind=kLoop, calls=%fused_computation.3 | loop fusion | flops 42462720 | bytes 44273664 | tf_op jit(solution)/shard_map/while/body/eval_jaxpr/reduce_sum | solution.py:146
  501.4 40.8 %reduce-scatter.21.cloned.1.call-done = f32[384,768]{1,0:T(8,128)} async-done(((f32[768,768]{1,0:T(8,128)}), f32[384,768]{1,0:T(8,128)}) %reduce-scatter.21.cloned.1.call-update) | async-done | bytes 1179664 | tf_op jit(solution)/shard_map/reduce_scatter | solution.py:118
  567.8 19.4 %all-gather.23.cloned.1.call-done = bf16[1,768,1536]{2,1,0:T(8,128)(2,1)} async-done(((bf16[1,48,1536]{2,1,0:T(8,128)(2,1)}), bf16[1,768,1536]{2,1,0:T(8,128)(2,1)}) %all-gather.23.cloned.1.call-update) | async-done | bytes 2359312 | tf_op jit(solution)/shard_map/all_gather | solution.py:86
  594.0 36.5 %all-gather.25.cloned.1.call-done = bf16[1,1536,768]{2,1,0:T(8,128)(2,1)} async-done(((bf16[1,96,768]{2,1,0:T(8,128)(2,1)}), bf16[1,1536,768]{2,1,0:T(8,128)(2,1)}) %all-gather.25.cloned.1.call-update) | async-done | bytes 2359312 | tf_op jit(solution)/shard_map/all_gather | solution.py:87
  647.9 27.6 %reduce-scatter.25.cloned.1.call-done = f32[384,768]{1,0:T(8,128)} async-done(((f32[768,768]{1,0:T(8,128)}), f32[384,768]{1,0:T(8,128)}) %reduce-scatter.25.cloned.1.call-update) | async-done | bytes 1179664 | tf_op jit(solution)/shard_map/reduce_scatter | solution.py:118
  679.4 33.1 %reduce-scatter.23.cloned.1.call-done = f32[384,768]{1,0:T(8,128)} async-done(((f32[768,768]{1,0:T(8,128)}), f32[384,768]{1,0:T(8,128)}) %reduce-scatter.23.cloned.1.call-update) | async-done | bytes 1179664 | tf_op jit(solution)/shard_map/reduce_scatter | solution.py:118
  736.6 19.4 %convolution_bitcast_fusion.1 = f32[2304,1,6,64]{0,3,2,1:T(8,128)} fusion(bf16[768,6,64]{0,2,1:T(8,128)(2,1)S(1)} %bitcast.280, f32[6,768,2304]{2,1,0:T(8,128)} %get-tuple-element.220, f32[6,768]{1,0:T(8,128)S(1)} %copy-done.89, pred[768,2304]{1,0:T(8,128)(4,1)S(1)} %fusion.7), kind=kOutput, calls=%fused_computation.40 | convolution fusion | flops 1401421824 | bytes 48384000 | tf_op jit(solution)/shard_map/while/body/eval_jaxpr/hqk,qhd->khd/dot_general | solution.py:183
  756.0 28.1 %multiply_convert_fusion.1 = bf16[6,768,2304]{2,1,0:T(8,128)(2,1)} fusion(f32[6,768,2304]{2,1,0:T(8,128)} %get-tuple-element.220, bf16[768,6,64]{0,2,1:T(8,128)(2,1)S(1)} %bitcast.281, f32[6,768]{1,0:T(8,128)S(1)} %bitcast.291, f32[6,768]{1,0:T(8,128)S(1)} %copy-done.89, pred[768,2304]{1,0:T(8,128)(4,1)S(1)} %fusion.7, ...), kind=kOutput, calls=%fused_computation.1 | convolution fusion | flops 1422655488 | bytes 67866624 | tf_op jit(solution)/shard_map/while/body/eval_jaxpr/qhd,khd->hqk/dot_general | solution.py:170
  835.6 39.7 %reduce-scatter.27.cloned.1.call-done = f32[384,768]{1,0:T(8,128)} async-done(((f32[768,768]{1,0:T(8,128)}), f32[384,768]{1,0:T(8,128)}) %reduce-scatter.27.cloned.1.call-update) | async-done | bytes 1179664 | tf_op jit(solution)/shard_map/reduce_scatter | solution.py:118
  909.5 34.9 %reduce-scatter.29.cloned.1.call-done = f32[384,768]{1,0:T(8,128)} async-done(((f32[768,768]{1,0:T(8,128)}), f32[384,768]{1,0:T(8,128)}) %reduce-scatter.29.cloned.1.call-update) | async-done | bytes 1179664 | tf_op jit(solution)/shard_map/reduce_scatter | solution.py:118
  969.3 19.6 %convolution_bitcast_fusion = f32[2304,1,6,64]{0,3,2,1:T(8,128)} fusion(bf16[768,6,64]{0,2,1:T(8,128)(2,1)S(1)} %bitcast.277, f32[6,768,2304]{2,1,0:T(8,128)} %get-tuple-element.216, f32[6,768]{1,0:T(8,128)S(1)} %copy-done.88, pred[768,2304]{1,0:T(8,128)(4,1)S(1)} %fusion.7), kind=kOutput, calls=%fused_computation.39 | convolution fusion | flops 1401421824 | bytes 48384000 | tf_op jit(solution)/shard_map/while/body/eval_jaxpr/hqk,qhd->khd/dot_general | solution.py:183
  988.9 28.1 %multiply_convert_fusion = bf16[6,768,2304]{2,1,0:T(8,128)(2,1)} fusion(f32[6,768,2304]{2,1,0:T(8,128)} %get-tuple-element.216, bf16[768,6,64]{0,2,1:T(8,128)(2,1)S(1)} %bitcast.278, f32[6,768]{1,0:T(8,128)S(1)} %bitcast.290, f32[6,768]{1,0:T(8,128)S(1)} %copy-done.88, pred[768,2304]{1,0:T(8,128)(4,1)S(1)} %fusion.7, ...), kind=kOutput, calls=%fused_computation | convolution fusion | flops 1422655488 | bytes 67866624 | tf_op jit(solution)/shard_map/while/body/eval_jaxpr/qhd,khd->hqk/dot_general | solution.py:170
  1143.2 25.0 %reduce-scatter.39.cloned.1.call-done = f32[24,768]{1,0:T(8,128)} async-done(((f32[384,768]{1,0:T(8,128)}), f32[24,768]{1,0:T(8,128)}) %reduce-scatter.39.cloned.1.call-update) | async-done | bytes 73744 | tf_op jit(solution)/shard_map/reduce_scatter | solution.py:360
  1168.1 60.8 %reduce-scatter.37.cloned.1.call-done = f32[24,768]{1,0:T(8,128)} async-done(((f32[384,768]{1,0:T(8,128)}), f32[24,768]{1,0:T(8,128)}) %reduce-scatter.37.cloned.1.call-update) | async-done | bytes 73744 | tf_op jit(solution)/shard_map/reduce_scatter | solution.py:360
  1230.5 76.8 %reduce-scatter.47.cloned.1.call-done = f32[96,768]{1,0:T(8,128)} async-done(((f32[1536,768]{1,0:T(8,128)}), f32[96,768]{1,0:T(8,128)}) %reduce-scatter.47.cloned.1.call-update) | async-done | bytes 294928 | tf_op jit(solution)/shard_map/reduce_scatter | solution.py:362
  1307.3 78.5 %reduce-scatter.45.cloned.1.call-done = f32[96,768]{1,0:T(8,128)} async-done(((f32[1536,768]{1,0:T(8,128)}), f32[96,768]{1,0:T(8,128)}) %reduce-scatter.45.cloned.1.call-update) | async-done | bytes 294928 | tf_op jit(solution)/shard_map/reduce_scatter | solution.py:362
  1387.7 76.7 %reduce-scatter.43.cloned.1.call-done = f32[48,1536]{1,0:T(8,128)} async-done(((f32[768,1536]{1,0:T(8,128)}), f32[48,1536]{1,0:T(8,128)}) %reduce-scatter.43.cloned.1.call-update) | async-done | bytes 294928 | tf_op jit(solution)/shard_map/reduce_scatter | solution.py:361
  1464.5 78.5 %reduce-scatter.41.cloned.1.call-done = f32[48,1536]{1,0:T(8,128)} async-done(((f32[768,1536]{1,0:T(8,128)}), f32[48,1536]{1,0:T(8,128)}) %reduce-scatter.41.cloned.1.call-update) | async-done | bytes 294928 | tf_op jit(solution)/shard_map/reduce_scatter | solution.py:361
  1547.0 128.6 %all-reduce.3.cloned.1.call-done = (f32[1,2,768]{2,1,0:T(2,128)}, f32[1,2,768]{2,1,0:T(2,128)}, f32[1,3072]{1,0:T(1,128)}, f32[1,3072]{1,0:T(1,128)}, f32[1,2,76...) async-done(((f32[1,2,768]{2,1,0:T(2,128)}, f32[1,2,768]{2,1,0:T(2,128)}, ...) | async-done | bytes 73744 | tf_op jit(solution)/shard_map/psum | solution.py:364
  1682.2 68.5 %reduce-scatter.35.cloned.1.call-done = f32[48,3,384]{2,0,1:T(8,128)} async-done(((f32[768,3,384]{2,0,1:T(8,128)}), f32[48,3,384]{2,0,1:T(8,128)}) %reduce-scatter.35.cloned.1.call-update) | async-done | bytes 221200 | tf_op jit(solution)/shard_map/reduce_scatter | solution.py:359
  1750.7 70.9 %reduce-scatter.33.cloned.1.call-done = f32[48,3,384]{2,0,1:T(8,128)} async-done(((f32[768,3,384]{2,0,1:T(8,128)}), f32[48,3,384]{2,0,1:T(8,128)}) %reduce-scatter.33.cloned.1.call-update) | async-done | bytes 221200 | tf_op jit(solution)/shard_map/reduce_scatter | solution.py:359
  (470 shorter events, 483.1 us)
Async XLA Ops:
  7.2 46.8 %all-gather.15.cloned.1.call-start = ((), (), s32[]{:S(2)}) async-start(), calls=%async_computation.32 | async-start | bytes 1880064 | tf_op jit(solution)/shard_map/all_gather | solution.py:84
  9.0 200.2 %reduce-scatter.17.cloned.1.call-start = ((), (), s32[]{:S(2)}) async-start(), calls=%async_computation.16 | async-start | bytes 3538944 | tf_op jit(solution)/shard_map/reduce_scatter | solution.py:118
  61.8 48.8 %collective-permute-start.2 = (bf16[768,768]{0,1:T(8,128)(2,1)}, bf16[768,768]{0,1:T(8,128)(2,1)}, u32[]{:S(2)}, u32[]{:S(2)}) collective-permute-start(bf16[768,768]{0,1:T(8,128)(2,1)} %bitcast.6), channel_id=1, source_target_pairs={{2,0},{4,2},{6,4},{8,6},{10,8},{12,10},{14,12},{16,14},{18,16},{20... | collective-permute-start | bytes 3538952 | tf_op jit(solution)/shard_map/ppermute | solution.py:18
  63.1 47.5 %collective-permute-start.1 = (bf16[768,768]{0,1:T(8,128)(2,1)}, bf16[768,768]{0,1:T(8,128)(2,1)}, u32[]{:S(2)}, u32[]{:S(2)}) collective-permute-start(bf16[768,768]{0,1:T(8,128)(2,1)} %bitcast.6), channel_id=1, source_target_pairs={{0,2},{2,4},{4,6},{6,8},{8,10},{10,12},{12,14},{14,16},{16,18},{18... | collective-permute-start | bytes 3538952 | tf_op jit(solution)/shard_map/ppermute | solution.py:15
  174.4 79.9 %all-gather.17.cloned.1.call-start = ((), (), s32[]{:S(2)}) async-start(), calls=%async_computation.33 | async-start | bytes 2506752 | tf_op jit(solution)/shard_map/all_gather | solution.py:86
  176.2 121.9 %all-gather.19.cloned.1.call-start = ((), (), s32[]{:S(2)}) async-start(), calls=%async_computation.34 | async-start | bytes 2506752 | tf_op jit(solution)/shard_map/all_gather | solution.py:87
  177.9 159.6 %reduce-scatter.19.cloned.1.call-start = ((), (), s32[]{:S(2)}) async-start(), calls=%async_computation.17 | async-start | bytes 3538944 | tf_op jit(solution)/shard_map/reduce_scatter | solution.py:118
  303.9 76.8 %all-gather.21.cloned.1.call-start = ((), (), s32[]{:S(2)}) async-start(), calls=%async_computation.35 | async-start | bytes 1880064 | tf_op jit(solution)/shard_map/all_gather | solution.py:84
  304.4 237.8 %reduce-scatter.21.cloned.1.call-start = ((), (), s32[]{:S(2)}) async-start(), calls=%async_computation.18 | async-start | bytes 3538944 | tf_op jit(solution)/shard_map/reduce_scatter | solution.py:118
  340.3 44.2 %collective-permute-start.4 = (bf16[384,768]{1,0:T(8,128)(2,1)S(1)}, bf16[384,768]{1,0:T(8,128)(2,1)S(1)}, u32[]{:S(2)}, u32[]{:S(2)}) collective-permute-start(bf16[384,768]{1,0:T(8,128)(2,1)S(1)} %add_convert_fusion.3), channel_id=1, source_target_pairs={{0,1},{1,0},{2,3},{3,2},{4,5},{5,4},{6,7},{7,6},{8,9},{9,8},{10,11... | collective-permute-start | bytes 1769480 | tf_op jit(solution)/shard_map/ppermute | solution.py:105
  389.5 44.6 %collective-permute-start.6 = (bf16[768,768]{0,1:T(8,128)(2,1)S(1)}, bf16[768,768]{0,1:T(8,128)(2,1)S(1)}, u32[]{:S(2)}, u32[]{:S(2)}) collective-permute-start(bf16[768,768]{0,1:T(8,128)(2,1)S(1)} %bitcast.265), channel_id=1, source_target_pairs={{2,0},{4,2},{6,4},{8,6},{10,8},{12,10},{14,12},{16,14},{18,16},{20... | collective-permute-start | bytes 3538952 | tf_op jit(solution)/shard_map/ppermute | solution.py:18
  390.8 43.3 %collective-permute-start.5 = (bf16[768,768]{0,1:T(8,128)(2,1)S(1)}, bf16[768,768]{0,1:T(8,128)(2,1)S(1)}, u32[]{:S(2)}, u32[]{:S(2)}) collective-permute-start(bf16[768,768]{0,1:T(8,128)(2,1)S(1)} %bitcast.266), channel_id=1, source_target_pairs={{0,2},{2,4},{4,6},{6,8},{8,10},{10,12},{12,14},{14,16},{16,18},{18... | collective-permute-start | bytes 3538952 | tf_op jit(solution)/shard_map/ppermute | solution.py:15
  494.6 92.5 %all-gather.23.cloned.1.call-start = ((), (), s32[]{:S(2)}) async-start(), calls=%async_computation.36 | async-start | bytes 2506752 | tf_op jit(solution)/shard_map/all_gather | solution.py:86
  495.4 135.1 %all-gather.25.cloned.1.call-start = ((), (), s32[]{:S(2)}) async-start(), calls=%async_computation.37 | async-start | bytes 2506752 | tf_op jit(solution)/shard_map/all_gather | solution.py:87
  496.1 179.3 %reduce-scatter.25.cloned.1.call-start = ((), (), s32[]{:S(2)}) async-start(), calls=%async_computation.20 | async-start | bytes 3538944 | tf_op jit(solution)/shard_map/reduce_scatter | solution.py:118
  499.9 45.5 %collective-permute-start.8 = (bf16[384,768]{1,0:T(8,128)(2,1)}, bf16[384,768]{1,0:T(8,128)(2,1)}, u32[]{:S(2)}, u32[]{:S(2)}) collective-permute-start(bf16[384,768]{1,0:T(8,128)(2,1)} %get-tuple-element.199), channel_id=1, source_target_pairs={{0,1},{1,0},{2,3},{3,2},{4,5},{5,4},{6,7},{7,6},{8,9},{9,8},{10,11... | collective-permute-start | bytes 1769480 | tf_op jit(solution)/shard_map/ppermute | solution.py:105
  641.8 70.8 %reduce-scatter.23.cloned.1.call-start = ((), (), s32[]{:S(2)}) async-start(), calls=%async_computation.19 | async-start | bytes 3538944 | tf_op jit(solution)/shard_map/reduce_scatter | solution.py:118
  647.7 227.6 %reduce-scatter.27.cloned.1.call-start = ((), (), s32[]{:S(2)}) async-start(), calls=%async_computation.21 | async-start | bytes 3538944 | tf_op jit(solution)/shard_map/reduce_scatter | solution.py:118
  801.4 24.8 %collective-permute-start.11 = (bf16[768,768]{1,0:T(8,128)(2,1)}, bf16[768,768]{1,0:T(8,128)(2,1)}, u32[]{:S(2)}, u32[]{:S(2)}) collective-permute-start(bf16[768,768]{1,0:T(8,128)(2,1)} %copy.38), channel_id=1, source_target_pairs={{2,0},{4,2},{6,4},{8,6},{10,8},{12,10},{14,12},{16,14},{18,16},{20... | collective-permute-start | bytes 3538952 | tf_op jit(solution)/shard_map/ppermute | solution.py:26
  835.5 108.9 %reduce-scatter.29.cloned.1.call-start = ((), (), s32[]{:S(2)}) async-start(), calls=%async_computation.22 | async-start | bytes 3538944 | tf_op jit(solution)/shard_map/reduce_scatter | solution.py:118
  909.5 214.8 %reduce-scatter.31.cloned.1.call-start = ((), (), s32[]{:S(2)}) async-start(), calls=%async_computation.23 | async-start | bytes 3538944 | tf_op jit(solution)/shard_map/reduce_scatter | solution.py:118
  1033.4 25.1 %collective-permute-start.15 = (bf16[768,768]{1,0:T(8,128)(2,1)}, bf16[768,768]{1,0:T(8,128)(2,1)}, u32[]{:S(2)}, u32[]{:S(2)}) collective-permute-start(bf16[768,768]{1,0:T(8,128)(2,1)} %copy.42), channel_id=1, source_target_pairs={{2,0},{4,2},{6,4},{8,6},{10,8},{12,10},{14,12},{16,14},{18,16},{20... | collective-permute-start | bytes 3538952 | tf_op jit(solution)/shard_map/ppermute | solution.py:26
  1034.7 23.8 %collective-permute-start.14 = (bf16[768,768]{1,0:T(8,128)(2,1)}, bf16[768,768]{1,0:T(8,128)(2,1)}, u32[]{:S(2)}, u32[]{:S(2)}) collective-permute-start(bf16[768,768]{1,0:T(8,128)(2,1)} %copy.40), channel_id=1, source_target_pairs={{0,2},{2,4},{4,6},{6,8},{8,10},{10,12},{12,14},{14,16},{16,18},{18... | collective-permute-start | bytes 3538952 | tf_op jit(solution)/shard_map/ppermute | solution.py:26
  1067.1 101.0 %reduce-scatter.39.cloned.1.call-start = ((), (), s32[]{:S(2)}) async-start(), calls=%async_computation.27 | async-start | bytes 1253376 | tf_op jit(solution)/shard_map/reduce_scatter | solution.py:360
  1070.2 158.7 %reduce-scatter.37.cloned.1.call-start = ((), (), s32[]{:S(2)}) async-start(), calls=%async_computation.26 | async-start | bytes 1253376 | tf_op jit(solution)/shard_map/reduce_scatter | solution.py:360
  1072.0 235.3 %reduce-scatter.47.cloned.1.call-start = ((), (), s32[]{:S(2)}) async-start(), calls=%async_computation.31 | async-start | bytes 5013504 | tf_op jit(solution)/shard_map/reduce_scatter | solution.py:362
  1078.0 307.9 %reduce-scatter.45.cloned.1.call-start = ((), (), s32[]{:S(2)}) async-start(), calls=%async_computation.30 | async-start | bytes 5013504 | tf_op jit(solution)/shard_map/reduce_scatter | solution.py:362
  1084.4 380.1 %reduce-scatter.43.cloned.1.call-start = ((), (), s32[]{:S(2)}) async-start(), calls=%async_computation.29 | async-start | bytes 5013504 | tf_op jit(solution)/shard_map/reduce_scatter | solution.py:361
  1090.7 452.3 %reduce-scatter.41.cloned.1.call-start = ((), (), s32[]{:S(2)}) async-start(), calls=%async_computation.28 | async-start | bytes 5013504 | tf_op jit(solution)/shard_map/reduce_scatter | solution.py:361
  1096.9 578.7 %all-reduce.3.cloned.1.call-start = ((), (), s32[]{:S(2)}) async-start(), calls=%async_computation.38 | async-start | bytes 147456 | tf_op jit(solution)/shard_map/psum | solution.py:364
  1128.1 622.6 %reduce-scatter.35.cloned.1.call-start = ((), (), s32[]{:S(2)}) async-start(), calls=%async_computation.25 | async-start | bytes 3760128 | tf_op jit(solution)/shard_map/reduce_scatter | solution.py:359
  1133.0 688.6 %reduce-scatter.33.cloned.1.call-start = ((), (), s32[]{:S(2)}) async-start(), calls=%async_computation.24 | async-start | bytes 3760128 | tf_op jit(solution)/shard_map/reduce_scatter | solution.py:359
  (117 other events, 3004.8 us)
Sparse Core Ops, SparseCore 0:
  10.9 43.0 all-gather.14
  174.5 34.7 reduce-scatter.16
  212.1 42.0 all-gather.16
  257.0 41.0 all-gather.18
  304.0 33.5 reduce-scatter.18
  340.3 40.3 all-gather.20
  494.8 47.3 reduce-scatter.20
  545.1 42.0 all-gather.22
  589.4 41.0 all-gather.24
  641.9 33.5 reduce-scatter.24
  677.7 34.7 reduce-scatter.22
  835.7 39.5 reduce-scatter.26
  909.6 34.7 reduce-scatter.28
  1067.2 39.2 reduce-scatter.30
  1110.0 58.0 reduce-scatter.38
  1171.6 57.2 reduce-scatter.36
  1232.6 74.6 reduce-scatter.46
  1311.0 74.7 reduce-scatter.44
  1389.7 74.7 reduce-scatter.42
  1468.2 74.7 reduce-scatter.40
  1550.6 124.9 all-reduce.2
  1679.5 71.1 reduce-scatter.34
  1754.6 66.9 reduce-scatter.32
